TPU v7x, 32 devices: a whole 2x2x4 slice. The times are simulated.
32 devices in a mesh: seq: 8 (over z, y), mp: 4 (over x, core).
Axes of the slice: x: 2, y: 2, z: 4, core: 2. Of those that a mesh axis runs over, the one named last changes fastest.
Arguments:
- tokens: bfloat16 [16384, 2048], P('seq'), may hold values from -6 to 6
- w_proj: bfloat16 [2048, 4, 2048], P(None, None, 'mp')
- gain: float32 [2048], P('mp'), may hold values from 0.25 to 1.75
- level_codes: int32 [9, 16, 16384], P(None, 'mp', 'seq'), may hold values from 0 to 255
- w_codes: int32 [2048, 2048], P('mp'), may hold values from 40 to 199, as said below
- block_exponent: int32 [16, 16], P('mp'), may hold values from -7 to -5
Outputs:
- mixed: bfloat16 [16384, 2048], P(('seq', 'mp'))
Inputs may be any that keep to these rules, and one draw needn't show every extreme that they name: `w_codes`: each code is 128 s + 8 e + m with s of 0 or 1, e from 5 to 8 and m from 0 to 7.
All inputs are finite; a program needn't handle non-finite values.
Results may differ from a plain program's by a relative error of at most 0.015.
Values may be sent and summed in bfloat16 or wider, within the bound.
A program may use at most 128 MiB of HBM per device.

v0:
```python
import functools
import math

import jax
import jax.numpy as jnp
from jax import lax
from jax.experimental import pallas as pl
from jax.experimental.pallas import tpu as pltpu
from jax.sharding import PartitionSpec as P

HEAD_DIM = 128
STRETCH = 64
BLOCK = 128
CORES = 2
QB = 256
MESH = pl.DeviceIdType.MESH
F32 = jnp.float32
BF16 = jnp.bfloat16


def dot(a, b):
    return jnp.dot(a, b, preferred_element_type=F32)


def dot_nt(a, b):
    return lax.dot_general(a, b, (((1,), (1,)), ((), ())), preferred_element_type=F32)


def dot_tn(a, b):
    return lax.dot_general(a, b, (((0,), (0,)), ((), ())), preferred_element_type=F32)


def kernel(
    cfg,
    tok_hbm, w_hbm, codes_hbm, gain_ref, lw_ref, scale_ref,
    out_ref,
    tok, wj, wstage, cstage, wfull, kv, q, gate, att, attr, local, tot, snd, rcv, masks, acc,
    tok_sem, w_sem, c_sem, ws_sem, wr_sem, as_sem, ar_sem, ss_sem, sr_sem,
):
    groups, seq_bits, block_bits, in_bits, factors = cfg
    rows_all, width = q.shape
    depth = tok.shape[1]
    heads = width // HEAD_DIM
    rows = rows_all // groups
    chips = groups // CORES
    seq = lax.axis_index("seq")
    mp = lax.axis_index("mp")
    x = mp // CORES
    c = mp % CORES

    def peer(ix, kc):
        return ((x + ix) % chips) * CORES + (c + kc) % CORES

    def source(ix, kc):
        return ((x - ix + chips) % chips) * CORES + (c - kc + CORES) % CORES

    def seq_peer(j):
        bit = (seq // 2**j) % 2
        return seq + 2**j - bit * 2 ** (j + 1)

    crows = cstage.shape[1]
    wrows = wstage.shape[1]
    n_c = width // crows
    n_w = depth // wrows

    def c_copy(i):
        slot = i % 2
        return pltpu.make_async_copy(
            codes_hbm.at[pl.ds(i * crows, crows)], cstage.at[slot], c_sem.at[slot]
        )

    def w_copy(i):
        slot = i % 2
        return pltpu.make_async_copy(
            w_hbm.at[pl.ds(i * wrows, wrows)], wstage.at[slot], w_sem.at[slot]
        )

    for i in range(2):
        c_copy(i).start()
    for i in range(2):
        w_copy(i).start()
    tok_copy = pltpu.make_async_copy(tok_hbm, tok, tok_sem)
    tok_copy.start()

    barrier = pltpu.get_barrier_semaphore()
    for r in range(1, groups):
        pl.semaphore_signal(
            barrier, inc=1, device_id=(seq, peer(r // CORES, r % CORES)), device_id_type=MESH
        )
    for j in range(seq_bits):
        pl.semaphore_signal(barrier, inc=1, device_id=(seq_peer(j), mp), device_id_type=MESH)

    @pl.loop(0, n_c)
    def _(i):
        c_copy(i).wait()
        codes = cstage[i % 2]
        whole = ((codes & 7) | 8) << ((codes >> 3) & 15)
        value = whole.astype(F32)
        value = jnp.where(codes >= 128, -value, value)
        at = pl.ds(pl.multiple_of(i * crows, crows), crows)
        for k in range(depth // BLOCK):
            scale = jnp.left_shift(jnp.int32(1), scale_ref[i, k] + 16).astype(F32) * 2.0**-26
            cols = slice(k * BLOCK, (k + 1) * BLOCK)
            wfull[mp, at, cols] = (value[:, cols] * scale).astype(BF16)

        @pl.when(i + 2 < n_c)
        def _():
            c_copy(i + 2).start()

    hb = QB // 2
    t = lax.broadcasted_iota(jnp.int32, (hb, hb), 1)
    s = lax.broadcasted_iota(jnp.int32, (hb, hb), 0)
    tc = t // STRETCH
    sc = s // STRETCH
    masks[0] = jnp.where((tc == sc) & (s <= t), 1.0, 0.0).astype(F32)
    for j in range(in_bits - 1):
        hit = ((tc // 2**j) % 2 == 1) & (sc // 2**j == tc // 2**j - 1)
        masks[j + 1] = jnp.where(hit, 1.0, 0.0).astype(F32)

    pl.semaphore_wait(barrier, groups - 1 + seq_bits)

    n_x = chips - 1
    parity = seq % 2
    half = width // 2
    piece = half // 2

    def w_send(k, shard, start, size, seq_to, mp_to):
        at = pl.ds(pl.multiple_of(start, piece), size)
        return pltpu.make_async_remote_copy(
            src_ref=wfull.at[shard, at], dst_ref=wfull.at[shard, at],
            send_sem=ws_sem.at[k], recv_sem=wr_sem.at[k],
            device_id=(seq_to, mp_to), device_id_type=MESH,
        )

    def x_part(ix, ch, shard):
        return w_send(2 * (ix - 1) + ch, shard, parity * half + ch * piece, piece, seq, peer(ix, 0))

    def y_part(ix, ch, which):
        k = 2 * n_x + 2 * (ix - 1) + ch
        return w_send(k, source(ix, 0), which * half + ch * piece, piece, seq_peer(0), mp)

    def cx_part(ix, ch, kc):
        k = 4 * n_x + 2 * (ix - 1) + ch
        return w_send(k, source(ix, kc), parity * half + ch * piece, piece, seq, peer(0, 1))

    def cy_part(ix, kc):
        return w_send(6 * n_x + ix - 1, source(ix, kc), (1 - parity) * half, half, seq, peer(0, 1))

    def c_part(shard):
        return w_send(7 * n_x, shard, 0, width, seq, peer(0, 1))

    def relay(ch):
        for ix in range(1, chips):
            x_part(ix, ch, source(ix, 0)).wait_recv()
            y_part(ix, ch, parity).start()
            cx_part(ix, ch, 0).start()

    for ch in range(2):
        for ix in range(1, chips):
            x_part(ix, ch, mp).start()
    c_part(mp).start()

    @pl.loop(0, n_w)
    def _(i):
        w_copy(i).wait()
        wj[:, pl.ds(pl.multiple_of(i * wrows, wrows), wrows), :] = jnp.swapaxes(wstage[i % 2], 0, 1)

        @pl.when(i + 2 < n_w)
        def _():
            w_copy(i + 2).start()

    tok_copy.wait()
    tb = min(512, rows_all)
    n_t = rows_all // tb

    @pl.loop(0, 2 * n_t)
    def _(i):
        part = i // n_t
        at = pl.ds(pl.multiple_of((i % n_t) * tb, tb), tb)
        kv[part, at, :] = dot(tok[at, :], wj[1 + part]).astype(BF16)

    n_b = rows_all // QB

    @pl.loop(0, heads)
    def _(h):
        cols = pl.ds(pl.multiple_of(h * HEAD_DIM, HEAD_DIM), HEAD_DIM)
        level = []
        for b in range(n_b):
            at = pl.ds(b * QB, QB)
            level.append(dot_tn(kv[1, at, cols], kv[0, at, cols]))
        base = 0
        while len(level) > 1:
            for b, state in enumerate(level):
                local[base + b, h] = state.astype(BF16)
            base += len(level)
            level = [level[2 * b] + level[2 * b + 1] for b in range(len(level) // 2)]
        tot[h] = level[0]
        snd[0, h] = level[0].astype(BF16)

    def s_send(j):
        return pltpu.make_async_remote_copy(
            src_ref=snd.at[j], dst_ref=rcv.at[j],
            send_sem=ss_sem.at[j], recv_sem=sr_sem.at[j],
            device_id=(seq_peer(j), mp), device_id_type=MESH,
        )

    s_send(0).start()

    def exchange(j):
        s_send(j).wait_recv()
        if j + 1 < seq_bits:
            total = tot[...] + rcv[j].astype(F32)
            tot[...] = total
            snd[j + 1] = total.astype(BF16)
            s_send(j + 1).start()

    in_loop = min(seq_bits - 1, n_t)

    @pl.loop(0, n_t)
    def _(i):
        at = pl.ds(pl.multiple_of(i * tb, tb), tb)
        q[at, :] = dot(tok[at, :], wj[0]).astype(BF16)
        g = dot(tok[at, :], wj[3])
        gate[at, :] = g / (1.0 + jnp.exp(-g)) * gain_ref[...]
        for j in range(in_loop):
            @pl.when(i == j)
            def _(j=j):
                exchange(j)
                if j == 0:
                    relay(0)

    if in_loop == 0:
        relay(0)
    relay(1)
    for j in range(in_loop, seq_bits):
        exchange(j)

    n_parts = rows // QB

    def a_send(r, target, part):
        at = pl.ds(pl.multiple_of(target * rows + part * QB, QB), QB)
        to = pl.ds(pl.multiple_of(part * QB, QB), QB)
        return pltpu.make_async_remote_copy(
            src_ref=att.at[at], dst_ref=attr.at[mp, to],
            send_sem=as_sem.at[r * n_parts + part], recv_sem=ar_sem.at[r * n_parts + part],
            device_id=(seq, target), device_id_type=MESH,
        )

    n_in = 1 + in_bits

    @pl.loop(0, groups)
    def _(step):
        r = groups - 1 - step
        owner = peer(r // CORES, r % CORES)

        @pl.loop(0, rows // QB)
        def _(part):
            b = owner * (rows // QB) + part
            at = pl.ds(pl.multiple_of(b * QB, QB), QB)
            for h in range(heads):
                cols = slice(h * HEAD_DIM, (h + 1) * HEAD_DIM)
                qh = q[at, cols]
                vh = kv[1, at, cols]

                def weight(level):
                    return lw_ref[level, h : h + 1, at].astype(F32) * factors[level]

                scores = dot_nt(kv[0, at, cols], qh)

                def corner(lo):
                    side = slice(lo, lo + hb)
                    mix = weight(0)[:, side] * masks[0]
                    for j in range(in_bits - 1):
                        mix = mix + weight(1 + j)[:, side] * masks[1 + j]
                    return (scores[side, side] * mix).astype(BF16)

                upper = (scores[:hb, hb:] * weight(in_bits)[:, hb:]).astype(BF16)
                probs = jnp.concatenate(
                    [
                        jnp.concatenate([corner(0), upper], 1),
                        jnp.concatenate([jnp.zeros((hb, hb), BF16), corner(hb)], 1),
                    ],
                    0,
                )
                qt = qh.astype(F32).T
                left = []
                right = []
                base = 0
                for j in range(block_bits):
                    node = b // 2**j
                    bit = node % 2
                    right.append((qt * (weight(n_in + j) * bit.astype(F32))).astype(BF16))
                    left.append(local[base + node - bit, h])
                    base += n_b >> j
                for j in range(seq_bits):
                    bit = (seq // 2**j) % 2
                    right.append((qt * (weight(n_in + block_bits + j) * bit.astype(F32))).astype(BF16))
                    left.append(rcv[j, h])
                memory = dot_tn(vh, probs) + dot(
                    jnp.concatenate(left, 1), jnp.concatenate(right, 0)
                )
                mean = jnp.mean(memory * memory, axis=0, keepdims=True)
                normed = (memory * lax.rsqrt(mean + 1e-06)).T
                att[at, cols] = (normed * gate[at, cols]).astype(BF16)

            @pl.when(r > 0)
            def _():
                a_send(r, owner, part).start()

    for ix in range(1, chips):
        for ch in range(2):
            y_part(ix, ch, 1 - parity).wait_recv()
        cy_part(ix, 0).start()

    nb = min(512, depth)

    def product(left, g, first, last):
        @pl.loop(0, depth // nb)
        def _(i):
            cols = pl.ds(pl.multiple_of(i * nb, nb), nb)
            value = dot(left, wfull[g, :, cols])
            if not first:
                value = value + acc[:, cols]
            if last:
                out_ref[:, cols] = value.astype(BF16)
            else:
                acc[:, cols] = value

    own = pl.ds(pl.multiple_of(mp * rows, rows), rows)
    product(att[own, :], mp, True, groups == 1)
    for r in range(1, groups):
        ix, kc = r // CORES, r % CORES
        src = source(ix, kc)
        for part in range(n_parts):
            to = pl.ds(part * QB, QB)
            k = r * n_parts + part
            pltpu.make_async_remote_copy(
                src_ref=attr.at[src, to], dst_ref=attr.at[src, to],
                send_sem=as_sem.at[k], recv_sem=ar_sem.at[k],
                device_id=(seq, src), device_id_type=MESH,
            ).wait_recv()
        if kc and ix:
            for ch in range(2):
                cx_part(ix, ch, 1).wait_recv()
            cy_part(ix, 1).wait_recv()
        elif kc:
            c_part(src).wait_recv()
        product(attr[src], src, False, r == groups - 1)

    c_part(mp).wait_send()
    for ix in range(1, chips):
        for ch in range(2):
            x_part(ix, ch, mp).wait_send()
            y_part(ix, ch, parity).wait_send()
            cx_part(ix, ch, 0).wait_send()
        cy_part(ix, 0).wait_send()
    for j in range(seq_bits):
        s_send(j).wait_send()
    for r in range(1, groups):
        for part in range(n_parts):
            a_send(r, peer(r // CORES, r % CORES), part).wait_send()


def body(tokens, w_proj, gain, level_codes, w_codes, block_exponent):
    rows_all, depth = tokens.shape
    width = w_proj.shape[2]
    heads = width // HEAD_DIM
    groups = lax.axis_size("mp")
    seq_size = lax.axis_size("seq")
    seq_bits = seq_size.bit_length() - 1
    stretch_bits = (rows_all // STRETCH).bit_length() - 1
    in_bits = (QB // STRETCH).bit_length() - 1
    block_bits = stretch_bits - in_bits
    levels = level_codes.shape[0]
    rows = rows_all // groups
    chips = groups // CORES
    spans = [STRETCH] + [STRETCH << j for j in range(levels - 1)]
    factors = [1.0 / 128.0 / math.sqrt(HEAD_DIM * span) for span in spans]
    n_b = rows_all // QB
    vmem = pl.BlockSpec(memory_space=pltpu.VMEM)
    hbm = pl.BlockSpec(memory_space=pl.ANY)
    dma = pltpu.SemaphoreType.DMA
    return pl.pallas_call(
        functools.partial(kernel, (groups, seq_bits, block_bits, in_bits, factors)),
        out_shape=jax.ShapeDtypeStruct((rows, depth), BF16),
        in_specs=[hbm, hbm, hbm, vmem, vmem, pl.BlockSpec(memory_space=pltpu.SMEM)],
        out_specs=vmem,
        scratch_shapes=[
            pltpu.VMEM((rows_all, depth), BF16),
            pltpu.VMEM((4, depth, width), BF16),
            pltpu.VMEM((2, 256, 4, width), BF16),
            pltpu.VMEM((2, BLOCK, depth), jnp.int32),
            pltpu.VMEM((groups, width, depth), BF16),
            pltpu.VMEM((2, rows_all, width), BF16),
            pltpu.VMEM((rows_all, width), BF16),
            pltpu.VMEM((rows_all, width), F32),
            pltpu.VMEM((rows_all, width), BF16),
            pltpu.VMEM((groups, rows, width), BF16),
            pltpu.VMEM((2 * n_b, heads, HEAD_DIM, HEAD_DIM), BF16),
            pltpu.VMEM((heads, HEAD_DIM, HEAD_DIM), F32),
            pltpu.VMEM((seq_bits, heads, HEAD_DIM, HEAD_DIM), BF16),
            pltpu.VMEM((seq_bits, heads, HEAD_DIM, HEAD_DIM), BF16),
            pltpu.VMEM((in_bits, QB // 2, QB // 2), F32),
            pltpu.VMEM((rows, depth), F32),
            dma, dma((2,)), dma((2,)),
            dma((7 * chips - 6,)), dma((7 * chips - 6,)),
            dma((groups * (rows // QB),)), dma((groups * (rows // QB),)),
            dma((seq_bits,)), dma((seq_bits,)),
        ],
        compiler_params=pltpu.CompilerParams(
            collective_id=0, has_side_effects=True, vmem_limit_bytes=67043328
        ),
        name="layer",
    )(tokens, w_proj, w_codes, gain.reshape(1, width), level_codes, block_exponent)


def solution(mesh):
    placed = (
        P("seq", None),
        P(None, None, "mp"),
        P("mp"),
        P(None, "mp", "seq"),
        P("mp", None),
        P("mp", None),
    )
    return jax.shard_map(
        body, mesh=mesh, in_specs=placed, out_specs=P(("seq", "mp"), None), check_vma=False
    )
```

profile of v0, /device:TPU:0, one launch (start us, length us, event | category | flops | bytes accessed | tf_op | source)
XLA Modules:
  0.0 75.4 jit_solution(8713726808036135486)
XLA Ops:
  0.0 72.2 %layer.1 = bf16[512,2048]{1,0:T(8,128)(2,1)} custom-call(bf16[2048,2048]{1,0:T(8,128)(2,1)} %tok_hbm.1, bf16[2048,4,512]{2,1,0:T(4,128)(2,1)} %w_hbm.1, s32[512,2048]{1,0:T(8,128)} %codes_hbm.1, f32[1,512]{1,0:T(1,128)} %bitcast.1, s32[9,4,2048]{2,1,0:T(4,128)} %lw_ref.1, s32[4,16]{1,0:T(4,128)} %scale_ref.1), custom_call_target="tpu_custom_call" | custom-call | tf_op jit(solution)/shard_map/layer/pallas_call | solution.py:383
  72.2 3.2 %copy.8 = bf16[512,2048]{1,0:T(8,128)(2,1)} copy(bf16[512,2048]{1,0:T(8,128)(2,1)} %layer.1) | data formatting | bytes 4194304
where the time goes:
time: 75.6 us; the launch traced here: 75.4 us
  Pallas kernels  72.2 us (96%)
  local copies, waits for them, and re-layouts  3.16 us (4%)
    pallas_call x1, Pallas kernels, body(): pl.pallas_call(functools.partial(kernel, (groups, seq_bits, block_bits, i...  72.2 us
    unnamed x1, local copies, waits for them, and re-layouts  3.16 us

commit v1 on v0

v1 whole, which is shorter than its diff:
```python
import functools
import math

import jax
import jax.numpy as jnp
from jax import lax
from jax.experimental import pallas as pl
from jax.experimental.pallas import tpu as pltpu
from jax.sharding import PartitionSpec as P

HEAD_DIM = 128
STRETCH = 64
BLOCK = 128
CORES = 2
QB = 256
QUARTERS = 4
CHUNKS = 4
MESH = pl.DeviceIdType.MESH
F32 = jnp.float32
BF16 = jnp.bfloat16


def dot(a, b):
    return jnp.dot(a, b, preferred_element_type=F32)


def dot_nt(a, b):
    return lax.dot_general(a, b, (((1,), (1,)), ((), ())), preferred_element_type=F32)


def dot_tn(a, b):
    return lax.dot_general(a, b, (((0,), (0,)), ((), ())), preferred_element_type=F32)


def kernel(
    cfg,
    tok_hbm, w_hbm, codes_hbm, gain_hbm, lw_hbm, scale_ref,
    out_hbm,
    tok, wstage, cstage, wfull, kv, q, gate, att, attr, local, tot, snd, rcv, masks, acc, outv,
    lw_ref, gain_ref,
    tok_sem, w_sem, c_sem, in_sem, out_sem, ws_sem, wr_sem, as_sem, ar_sem, ss_sem, sr_sem,
    *wh,
):
    groups, seq_bits, block_bits, in_bits, factors = cfg
    rows_all, depth = tok.shape
    pairs = len(wh)
    heads, width = tot.shape[0], att.shape[1]
    hp = heads // pairs
    pw = hp * HEAD_DIM
    rows = rows_all // groups
    chips = groups // CORES
    n_parts = rows // QB
    n_b = rows_all // QB
    seq = lax.axis_index("seq")
    mp = lax.axis_index("mp")
    x = mp // CORES
    c = mp % CORES
    bit0 = seq % 2
    bit1 = (seq // 2) % 2

    def peer(ix, kc):
        return ((x + ix) % chips) * CORES + (c + kc) % CORES

    def source(ix, kc):
        return ((x - ix + chips) % chips) * CORES + (c - kc + CORES) % CORES

    def seq_peer(j):
        bit = (seq // 2**j) % 2
        return seq + 2**j - bit * 2 ** (j + 1)

    mine = bit1 * 2 + bit0
    over0 = bit1 * 2 + 1 - bit0
    over1 = (1 - bit1) * 2 + bit0
    over01 = (1 - bit1) * 2 + 1 - bit0

    crows = width // QUARTERS
    n_t = 4
    tb = rows_all // n_t
    wrows = depth // n_t

    def code_piece(i):
        return (mine + i) % QUARTERS

    def c_copy(i):
        at = pl.ds(pl.multiple_of(code_piece(i) * crows, crows), crows)
        return pltpu.make_async_copy(codes_hbm.at[at], cstage.at[i], c_sem.at[i])

    def w_copy(h, i):
        at = pl.ds(i * wrows, wrows)
        cols = pl.ds(h * pw, pw)
        return pltpu.make_async_copy(
            w_hbm.at[at, :, cols], wstage.at[h % 2, at], w_sem.at[h % 2, i]
        )

    def tok_copy(i):
        at = pl.ds(pl.multiple_of(i * tb, tb), tb)
        return pltpu.make_async_copy(tok_hbm.at[at], tok.at[at], tok_sem.at[i])

    c_copy(0).start()
    for i in range(n_t):
        w_copy(0, i).start()
    tok_copy(0).start()
    tok_copy(1).start()
    if pairs > 1:
        for i in range(n_t):
            w_copy(1, i).start()
    tok_copy(2).start()
    tok_copy(3).start()
    for i in range(1, QUARTERS):
        c_copy(i).start()
    lw_copy = pltpu.make_async_copy(lw_hbm, lw_ref, in_sem.at[0])
    gain_copy = pltpu.make_async_copy(gain_hbm, gain_ref, in_sem.at[1])
    lw_copy.start()
    gain_copy.start()

    barrier = pltpu.get_barrier_semaphore()
    for r in range(1, groups):
        pl.semaphore_signal(
            barrier, inc=1, device_id=(seq, peer(r // CORES, r % CORES)), device_id_type=MESH
        )
    for j in range(seq_bits):
        pl.semaphore_signal(barrier, inc=1, device_id=(seq_peer(j), mp), device_id_type=MESH)

    def decode(i, start, size):
        piece = code_piece(i)
        codes = cstage[i, pl.ds(start, size)]
        whole = ((codes & 7) | 8) << ((codes >> 3) & 15)
        value = whole.astype(F32)
        value = jnp.where(codes >= 128, -value, value)
        at = pl.ds(pl.multiple_of(piece * crows + start, 16), size)
        block = piece * crows // BLOCK
        for k in range(depth // BLOCK):
            scale = jnp.left_shift(jnp.int32(1), scale_ref[block, k] + 16).astype(F32) * 2.0**-26
            cols = slice(k * BLOCK, (k + 1) * BLOCK)
            wfull[mp, at, cols] = (value[:, cols] * scale).astype(BF16)

    def relayout(p, start, size):
        at = pl.ds(pl.multiple_of(start, size), size)
        piece = jnp.swapaxes(wstage[p % 2, at], 0, 1)
        wh[p][0, at, :pw] = piece[1]
        wh[p][0, at, pw:] = piece[2]
        wh[p][1, at, :pw] = piece[0]
        wh[p][1, at, pw:] = piece[3]

    csize = crows // CHUNKS

    def w_send(k, shard, start, size, seq_to, mp_to):
        at = pl.ds(pl.multiple_of(start, 16), size)
        return pltpu.make_async_remote_copy(
            src_ref=wfull.at[shard, at], dst_ref=wfull.at[shard, at],
            send_sem=ws_sem.at[k], recv_sem=wr_sem.at[k],
            device_id=(seq_to, mp_to), device_id_type=MESH,
        )

    n_x = chips - 1
    per = 4 * CHUNKS + 4

    def slot(ix, kind, ch):
        return (ix - 1) * per + kind * CHUNKS + ch

    def x_part(ix, ch, shard):
        return w_send(slot(ix, 0, ch), shard, mine * crows + ch * csize, csize, seq, peer(ix, 0))

    def y_part(ix, ch, quarter):
        at = quarter * crows + ch * csize
        return w_send(slot(ix, 1, ch), source(ix, 0), at, csize, seq_peer(0), mp)

    def z_part(ix, ch, quarter):
        at = quarter * crows + ch * csize
        return w_send(slot(ix, 2, ch), source(ix, 0), at, csize, seq_peer(1), mp)

    def d_part(ix, ch, quarter):
        at = quarter * crows + ch * csize
        return w_send(slot(ix, 3, ch), source(ix, 0), at, csize, seq_peer(0), mp)

    def core_part(ix, n, kc):
        quarter = (mine, over0, over1, over01)[n]
        k = slot(ix, 4, 0) + n
        return w_send(k, source(ix, kc), quarter * crows, crows, seq, peer(0, 1))

    def own_part(shard):
        return w_send(n_x * per, shard, 0, width, seq, peer(0, 1))

    remote = range(1, chips)

    def core_send(n):
        for ix in remote:
            core_part(ix, n, 0).start()

    def x_relay(ch):
        for ix in remote:
            x_part(ix, ch, source(ix, 0)).wait_recv()
            y_part(ix, ch, mine).start()
        if ch == CHUNKS - 1:
            core_send(0)

    def z_start(ch):
        for ix in remote:
            z_part(ix, ch, mine).start()

    def z_relay(ch):
        for ix in remote:
            z_part(ix, ch, over1).wait_recv()
            d_part(ix, ch, over1).start()
        if ch == CHUNKS - 1:
            core_send(2)

    def y_done():
        for ix in remote:
            for ch in range(CHUNKS):
                y_part(ix, ch, over0).wait_recv()
        core_send(1)

    def d_done():
        for ix in remote:
            for ch in range(CHUNKS):
                d_part(ix, ch, over01).wait_recv()
        core_send(3)

    def part_of(h, which):
        lo = which * pw + h % hp * HEAD_DIM
        return slice(lo, lo + HEAD_DIM)

    def states(h):
        level = []
        for b in range(n_b):
            at = pl.ds(b * QB, QB)
            level.append(dot_tn(kv[h // hp, at, part_of(h, 1)], kv[h // hp, at, part_of(h, 0)]))
        base = 0
        while len(level) > 1:
            for b, state in enumerate(level):
                local[base + b, h] = state.astype(BF16)
            base += len(level)
            level = [level[2 * b] + level[2 * b + 1] for b in range(len(level) // 2)]
        tot[h] = level[0]
        snd[0, h] = level[0].astype(BF16)

    def s_send(j, h):
        return pltpu.make_async_remote_copy(
            src_ref=snd.at[j, h], dst_ref=rcv.at[j, h],
            send_sem=ss_sem.at[j, h], recv_sem=sr_sem.at[j, h],
            device_id=(seq_peer(j), mp), device_id_type=MESH,
        )

    progress = [0] * heads

    def exchange(h):
        j = progress[h]
        s_send(j, h).wait_recv()
        if j + 1 < seq_bits:
            total = tot[h] + rcv[j, h].astype(F32)
            tot[h] = total
            snd[j + 1, h] = total.astype(BF16)
            s_send(j + 1, h).start()
        progress[h] += 1

    def advance(p, upto):
        for h in range(p * hp, (p + 1) * hp) if p < pairs else ():
            if progress[h] < min(upto, seq_bits - 1):
                exchange(h)

    def complete(h):
        while progress[h] < seq_bits:
            exchange(h)

    def query(p, first, last, after=None):
        @pl.loop(first, last)
        def _(step):
            r = groups - 1 - step
            owner = peer(r // CORES, r % CORES)
            at = pl.ds(pl.multiple_of(owner * rows, rows), rows)
            both = dot(tok[at, :], wh[p][1])
            q[p, at, :] = both[:, :pw].astype(BF16)
            g = both[:, pw:]
            gain = gain_ref[:, p * pw : (p + 1) * pw]
            gate[p, at, :] = g / (1.0 + jnp.exp(-g)) * gain
            if after:
                pl.when(step == first)(after)

    def a_send(r, target, part, h):
        at = pl.ds(pl.multiple_of(target * rows + part * QB, QB), QB)
        to = pl.ds(pl.multiple_of(part * QB, QB), QB)
        cols = pl.ds(h * HEAD_DIM, HEAD_DIM)
        k = (r * n_parts + part) * heads + h
        return pltpu.make_async_remote_copy(
            src_ref=att.at[at, cols], dst_ref=attr.at[mp, to, cols],
            send_sem=as_sem.at[k], recv_sem=ar_sem.at[k],
            device_id=(seq, target), device_id_type=MESH,
        )

    def a_wait(r, part, h):
        src = source(r // CORES, r % CORES)
        to = pl.ds(part * QB, QB)
        cols = pl.ds(h * HEAD_DIM, HEAD_DIM)
        k = (r * n_parts + part) * heads + h
        pltpu.make_async_remote_copy(
            src_ref=attr.at[src, to, cols], dst_ref=attr.at[src, to, cols],
            send_sem=as_sem.at[k], recv_sem=ar_sem.at[k],
            device_id=(seq, src), device_id_type=MESH,
        ).wait_recv()

    unit = 2
    hb = QB // 2
    n_in = 1 + in_bits

    def attend_block(h, b):
        cols = slice(h * HEAD_DIM, (h + 1) * HEAD_DIM)
        at = pl.ds(pl.multiple_of(b * QB, QB), QB)
        qh = q[h // hp, at, part_of(h, 0)]

        def weight(level):
            return lw_ref[level, h : h + 1, at].astype(F32) * factors[level]

        scores = dot_nt(kv[h // hp, at, part_of(h, 0)], qh)

        def corner(lo):
            side = slice(lo, lo + hb)
            mix = weight(0)[:, side] * masks[0]
            for j in range(in_bits - 1):
                mix = mix + weight(1 + j)[:, side] * masks[1 + j]
            return (scores[side, side] * mix).astype(BF16)

        upper = (scores[:hb, hb:] * weight(in_bits)[:, hb:]).astype(BF16)
        probs = jnp.concatenate(
            [
                jnp.concatenate([corner(0), upper], 1),
                jnp.concatenate([jnp.zeros((hb, hb), BF16), corner(hb)], 1),
            ],
            0,
        )
        qt = qh.astype(F32).T
        left = []
        right = []
        base = 0
        for j in range(block_bits):
            node = b // 2**j
            bit = node % 2
            right.append((qt * (weight(n_in + j) * bit.astype(F32))).astype(BF16))
            left.append(local[base + node - bit, h])
            base += n_b >> j
        for j in range(seq_bits):
            bit = (seq // 2**j) % 2
            right.append((qt * (weight(n_in + block_bits + j) * bit.astype(F32))).astype(BF16))
            left.append(rcv[j, h])
        memory = dot_tn(kv[h // hp, at, part_of(h, 1)], probs) + dot(
            jnp.concatenate(left, 1), jnp.concatenate(right, 0)
        )
        mean = jnp.mean(memory * memory, axis=0, keepdims=True)
        normed = (memory * lax.rsqrt(mean + 1e-06)).T
        att[at, cols] = (normed * gate[h // hp, at, part_of(h, 0)]).astype(BF16)

    def attend(p, first, last):
        pair = range(p * hp, (p + 1) * hp)
        span = last - first

        @pl.loop(0, n_parts * span // unit)
        def _(i):
            todo = []
            for k in range(unit):
                n = i * unit + k
                r = groups - 1 - first - n % span
                todo.append((r, peer(r // CORES, r % CORES), n // span))
            for r, owner, part in todo:
                for h in pair:
                    attend_block(h, owner * n_parts + part)
            for r, owner, part in todo:
                @pl.when(r > 0)
                def _():
                    for h in pair:
                        a_send(r, owner, part, h).start()

    nb = min(512, depth)

    c_copy(0).wait()
    decode(0, 0, crows)
    pl.semaphore_wait(barrier, groups - 1 + seq_bits)
    for ch in range(CHUNKS):
        for ix in remote:
            x_part(ix, ch, mp).start()
    for i in range(n_t):
        w_copy(0, i).wait()
        relayout(0, i * wrows, wrows)

    t = lax.broadcasted_iota(jnp.int32, (hb, hb), 1)
    s = lax.broadcasted_iota(jnp.int32, (hb, hb), 0)
    tc = t // STRETCH
    sc = s // STRETCH
    masks[0] = jnp.where((tc == sc) & (s <= t), 1.0, 0.0).astype(F32)
    for j in range(in_bits - 1):
        hit = ((tc // 2**j) % 2 == 1) & (sc // 2**j == tc // 2**j - 1)
        masks[j + 1] = jnp.where(hit, 1.0, 0.0).astype(F32)

    moves = {}
    for ch in range(CHUNKS):
        moves["x", ch] = functools.partial(x_relay, ch)
    for ch in range(CHUNKS):
        moves["z", ch] = functools.partial(z_start, ch)
    moves["y", 0] = y_done
    for ch in range(CHUNKS):
        moves["zr", ch] = functools.partial(z_relay, ch)
    moves["d", 0] = d_done

    def move(name, ch=0):
        step = moves.pop((name, ch), None)
        if step:
            step()

    half = n_t // 2
    sub = crows // n_t
    for p in range(pairs):
        last = p + 1 == pairs
        now = range(1, QUARTERS) if last else ()
        for i in now:
            c_copy(i).wait()

        def project(i):
            at = pl.ds(pl.multiple_of(i * tb, tb), tb)
            kv[p, at, :] = dot(tok[at, :], wh[p][0]).astype(BF16)
            for piece in now:
                decode(piece, i * sub, sub)

        @pl.loop(0, half)
        def _(i):
            if p == 0:
                tok_copy(i).wait()
            project(i)

        if p > 0:
            move("x", 1)
        if not last:
            for i in range(n_t):
                w_copy(p + 1, i).wait()

        @pl.loop(half, n_t)
        def _(i):
            if p == 0:
                tok_copy(i).wait()
            project(i)
            if not last:
                for k in range(4):
                    relayout(p + 1, (i - half) * 2 * wrows + k * wrows // 2, wrows // 2)
            if p > 0:
                @pl.when(i == half)
                def _():
                    advance(p - 1, 1)

        for h in range(p * hp, (p + 1) * hp):
            states(h)
            s_send(0, h).start()
        if p == 0:
            move("x", 0)
            move("z", 0)
        else:
            move("x", 2)
            move("x", 3)
    own_part(mp).start()

    lw_copy.wait()
    gain_copy.wait()
    n_far = groups - CORES
    query(0, 0, n_far, functools.partial(advance, 0, 2))
    if pairs > 1:
        query(1, 0, n_far, functools.partial(advance, 1, 1))
        move("z", 1)
    for h in range(hp):
        complete(h)
    attend(0, 0, n_far)
    advance(1, 2)
    for ch in range(CHUNKS):
        move("x", ch)
        move("z", ch)
    query(0, n_far, groups)
    move("y")
    move("zr", 0)
    if pairs > 1:
        query(1, n_far, groups)
        for h in range(hp, heads):
            complete(h)
        attend(1, 0, n_far)
    move("zr", 1)
    attend(0, n_far, groups)
    move("zr", 2)
    if pairs > 1:
        attend(1, n_far, groups)
    move("zr", 3)

    own = pl.ds(pl.multiple_of(mp * rows, rows), rows)
    partner = source(0, 1)
    for part in range(n_parts):
        for h in range(heads):
            a_wait(1, part, h)
    own_part(partner).wait_recv()

    @pl.loop(0, depth // nb)
    def _(i):
        cols = pl.ds(pl.multiple_of(i * nb, nb), nb)
        acc[:, cols] = dot(att[own, :], wfull[mp, :, cols]) + dot(
            attr[partner], wfull[partner, :, cols]
        )

    for name, ch in list(moves):
        move(name, ch)
    for ix in remote:
        for n in range(4):
            core_part(ix, n, 1).wait_recv()

    early = heads // 2
    cut = early * HEAD_DIM
    far = range(CORES, groups)
    for r in far:
        for part in range(n_parts):
            for h in range(early):
                a_wait(r, part, h)

    def far_sum(at, ks, cols):
        value = acc[at, cols]
        for r in far:
            src = source(r // CORES, r % CORES)
            value = value + dot(attr[src, at, ks], wfull[src, ks, cols])
        return value

    @pl.loop(0, depth // nb)
    def _(i):
        cols = pl.ds(pl.multiple_of(i * nb, nb), nb)
        acc[:, cols] = far_sum(slice(0, rows), slice(0, cut), cols)

    def out_copy(part):
        at = pl.ds(part * QB, QB)
        return pltpu.make_async_copy(outv.at[at], out_hbm.at[at], out_sem.at[part])

    for part in range(n_parts):
        for r in far:
            for h in range(early, heads):
                a_wait(r, part, h)
        at = slice(part * QB, (part + 1) * QB)

        @pl.loop(0, depth // nb)
        def _(i):
            cols = pl.ds(pl.multiple_of(i * nb, nb), nb)
            outv[at, cols] = far_sum(at, slice(cut, width), cols).astype(BF16)

        out_copy(part).start()

    own_part(mp).wait_send()
    for ix in remote:
        for ch in range(CHUNKS):
            x_part(ix, ch, mp).wait_send()
            y_part(ix, ch, mine).wait_send()
            z_part(ix, ch, mine).wait_send()
            d_part(ix, ch, over1).wait_send()
        for n in range(4):
            core_part(ix, n, 0).wait_send()
    for j in range(seq_bits):
        for h in range(heads):
            s_send(j, h).wait_send()
    for r in range(1, groups):
        for part in range(n_parts):
            for h in range(heads):
                a_send(r, peer(r // CORES, r % CORES), part, h).wait_send()
    for part in range(n_parts):
        out_copy(part).wait()


def body(tokens, w_proj, gain, level_codes, w_codes, block_exponent):
    rows_all, depth = tokens.shape
    width = w_proj.shape[2]
    heads = width // HEAD_DIM
    pw = 2 * HEAD_DIM
    pairs = width // pw
    groups = lax.axis_size("mp")
    seq_size = lax.axis_size("seq")
    seq_bits = seq_size.bit_length() - 1
    stretch_bits = (rows_all // STRETCH).bit_length() - 1
    in_bits = (QB // STRETCH).bit_length() - 1
    block_bits = stretch_bits - in_bits
    levels = level_codes.shape[0]
    rows = rows_all // groups
    chips = groups // CORES
    spans = [STRETCH] + [STRETCH << j for j in range(levels - 1)]
    factors = [1.0 / 128.0 / math.sqrt(HEAD_DIM * span) for span in spans]
    n_b = rows_all // QB
    hbm = pl.BlockSpec(memory_space=pl.ANY)
    dma = pltpu.SemaphoreType.DMA
    n_w = (chips - 1) * (4 * CHUNKS + 4) + 1
    n_a = groups * (rows // QB) * heads
    return pl.pallas_call(
        functools.partial(kernel, (groups, seq_bits, block_bits, in_bits, factors)),
        out_shape=jax.ShapeDtypeStruct((rows, depth), BF16),
        in_specs=[hbm, hbm, hbm, hbm, hbm, pl.BlockSpec(memory_space=pltpu.SMEM)],
        out_specs=hbm,
        scratch_shapes=[
            pltpu.VMEM((rows_all, depth), BF16),
            pltpu.VMEM((2, depth, 4, pw), BF16),
            pltpu.VMEM((QUARTERS, width // QUARTERS, depth), jnp.int32),
            pltpu.VMEM((groups, width, depth), BF16),
            pltpu.VMEM((pairs, rows_all, 2 * pw), BF16),
            pltpu.VMEM((pairs, rows_all, pw), BF16),
            pltpu.VMEM((pairs, rows_all, pw), F32),
            pltpu.VMEM((rows_all, width), BF16),
            pltpu.VMEM((groups, rows, width), BF16),
            pltpu.VMEM((2 * n_b, heads, HEAD_DIM, HEAD_DIM), BF16),
            pltpu.VMEM((heads, HEAD_DIM, HEAD_DIM), F32),
            pltpu.VMEM((seq_bits, heads, HEAD_DIM, HEAD_DIM), BF16),
            pltpu.VMEM((seq_bits, heads, HEAD_DIM, HEAD_DIM), BF16),
            pltpu.VMEM((in_bits, QB // 2, QB // 2), F32),
            pltpu.VMEM((rows, depth), F32),
            pltpu.VMEM((rows, depth), BF16),
            pltpu.VMEM(level_codes.shape, jnp.int32),
            pltpu.VMEM((1, width), F32),
            dma((4,)), dma((2, 4)), dma((QUARTERS,)), dma((2,)), dma((rows // QB,)),
            dma((n_w,)), dma((n_w,)),
            dma((n_a,)), dma((n_a,)),
            dma((seq_bits, heads)), dma((seq_bits, heads)),
        ]
        + [pltpu.VMEM((2, depth, 2 * pw), BF16)] * pairs,
        compiler_params=pltpu.CompilerParams(
            collective_id=0, has_side_effects=True, vmem_limit_bytes=67043328
        ),
        name="layer",
    )(tokens, w_proj, w_codes, gain.reshape(1, width), level_codes, block_exponent)


def solution(mesh):
    placed = (
        P("seq", None),
        P(None, None, "mp"),
        P("mp"),
        P(None, "mp", "seq"),
        P("mp", None),
        P("mp", None),
    )
    return jax.shard_map(
        body, mesh=mesh, in_specs=placed, out_specs=P(("seq", "mp"), None), check_vma=False
    )
```

time: 75.6 us -> 59.3 us (0.78)
  Pallas kernels: 72.2 us -> 55.9 us
    pallas_call x1, Pallas kernels: 72.2 us -> 55.9 us  [body(): pl.pallas_call(functools.partial(kernel, (groups, seq_bits, block_bits, i...]
where the time goes in v1:
time: 59.3 us; the launch traced here: 59.1 us
  Pallas kernels  55.9 us (94%)
  local copies, waits for them, and re-layouts  3.16 us (5%)
    pallas_call x1, Pallas kernels, body(): pl.pallas_call(functools.partial(kernel, (groups, seq_bits, block_bits, i...  55.9 us
    unnamed x1, local copies, waits for them, and re-layouts  3.16 us

profile of v1, /device:TPU:0, one launch (start us, length us, event | category | flops | bytes accessed | tf_op | source)
XLA Modules:
  0.0 59.1 jit_solution(12581276910650975008)
XLA Ops:
  0.0 55.9 %layer.1 = bf16[512,2048]{1,0:T(8,128)(2,1)} custom-call(bf16[2048,2048]{1,0:T(8,128)(2,1)} %tok_hbm.1, bf16[2048,4,512]{2,1,0:T(4,128)(2,1)} %w_hbm.1, s32[512,2048]{1,0:T(8,128)} %codes_hbm.1, f32[1,512]{1,0:T(1,128)} %bitcast.1, s32[9,4,2048]{2,1,0:T(4,128)} %lw_hbm.1, s32[4,16]{1,0:T(4,128)} %scale_ref.1), custom_call_target="tpu_custom_call" | custom-call | tf_op jit(solution)/shard_map/layer/pallas_call | solution.py:586
  56.0 3.2 %copy.8 = bf16[512,2048]{1,0:T(8,128)(2,1)} copy(bf16[512,2048]{1,0:T(8,128)(2,1)} %layer.1) | data formatting | bytes 4194304

commit v2 on v1

--- a/solution.py
+++ b/solution.py
@@ -35,10 +35,10 @@
 def kernel(
     cfg,
     tok_hbm, w_hbm, codes_hbm, gain_hbm, lw_hbm, scale_ref,
-    out_hbm,
-    tok, wstage, cstage, wfull, kv, q, gate, att, attr, local, tot, snd, rcv, masks, acc, outv,
+    outv,
+    tok, wstage, cstage, wfull, kv, q, gate, att, attr, local, tot, snd, rcv, masks, acc,
     lw_ref, gain_ref,
-    tok_sem, w_sem, c_sem, in_sem, out_sem, ws_sem, wr_sem, as_sem, ar_sem, ss_sem, sr_sem,
+    tok_sem, w_sem, c_sem, in_sem, ws_sem, wr_sem, as_sem, ar_sem, ss_sem, sr_sem,
     *wh,
 ):
     groups, seq_bits, block_bits, in_bits, factors = cfg
@@ -134,13 +134,12 @@
             cols = slice(k * BLOCK, (k + 1) * BLOCK)
             wfull[mp, at, cols] = (value[:, cols] * scale).astype(BF16)
 
-    def relayout(p, start, size):
+    def relayout(p, which, start, size):
         at = pl.ds(pl.multiple_of(start, size), size)
+        one, two = ((1, 2), (0, 3))[which]
         piece = jnp.swapaxes(wstage[p % 2, at], 0, 1)
-        wh[p][0, at, :pw] = piece[1]
-        wh[p][0, at, pw:] = piece[2]
-        wh[p][1, at, :pw] = piece[0]
-        wh[p][1, at, pw:] = piece[3]
+        wh[p][which, at, :pw] = piece[one]
+        wh[p][which, at, pw:] = piece[two]
 
     csize = crows // CHUNKS
 
@@ -371,15 +370,9 @@
 
     nb = min(512, depth)
 
-    c_copy(0).wait()
-    decode(0, 0, crows)
-    pl.semaphore_wait(barrier, groups - 1 + seq_bits)
-    for ch in range(CHUNKS):
-        for ix in remote:
-            x_part(ix, ch, mp).start()
     for i in range(n_t):
         w_copy(0, i).wait()
-        relayout(0, i * wrows, wrows)
+        relayout(0, 0, i * wrows, wrows)
 
     t = lax.broadcasted_iota(jnp.int32, (hb, hb), 1)
     s = lax.broadcasted_iota(jnp.int32, (hb, hb), 0)
@@ -412,6 +405,8 @@
         now = range(1, QUARTERS) if last else ()
         for i in now:
             c_copy(i).wait()
+        if p == 0:
+            c_copy(0).wait()
 
         def project(i):
             at = pl.ds(pl.multiple_of(i * tb, tb), tb)
@@ -419,14 +414,28 @@
             for piece in now:
                 decode(piece, i * sub, sub)
 
+        def rework(other, which, i):
+            for k in range(4):
+                relayout(other, which, i * 2 * wrows + k * wrows // 2, wrows // 2)
+
         @pl.loop(0, half)
         def _(i):
             if p == 0:
                 tok_copy(i).wait()
+                decode(0, i * (crows // half), crows // half)
             project(i)
-
-        if p > 0:
-            move("x", 1)
+            if p > 0:
+                rework(p - 1, 1, i)
+
+        if p == 0:
+            pl.semaphore_wait(barrier, groups - 1 + seq_bits)
+            for ch in range(CHUNKS):
+                for ix in remote:
+                    x_part(ix, ch, mp).start()
+        else:
+            advance(p - 1, 1)
+            move("x", 0)
+            move("z", 0)
         if not last:
             for i in range(n_t):
                 w_copy(p + 1, i).wait()
@@ -436,53 +445,52 @@
             if p == 0:
                 tok_copy(i).wait()
             project(i)
-            if not last:
-                for k in range(4):
-                    relayout(p + 1, (i - half) * 2 * wrows + k * wrows // 2, wrows // 2)
-            if p > 0:
-                @pl.when(i == half)
-                def _():
-                    advance(p - 1, 1)
+            if last:
+                rework(p, 1, i - half)
+            else:
+                rework(p + 1, 0, i - half)
 
         for h in range(p * hp, (p + 1) * hp):
             states(h)
             s_send(0, h).start()
-        if p == 0:
-            move("x", 0)
-            move("z", 0)
-        else:
-            move("x", 2)
-            move("x", 3)
+        if p > 0:
+            advance(p - 1, 2)
+            for ch in (1, 2):
+                move("x", ch)
+                move("z", ch)
     own_part(mp).start()
 
     lw_copy.wait()
     gain_copy.wait()
     n_far = groups - CORES
-    query(0, 0, n_far, functools.partial(advance, 0, 2))
+    query(0, 0, n_far)
+    for ch in range(CHUNKS):
+        move("x", ch)
+        move("z", ch)
+    move("zr", 0)
     if pairs > 1:
-        query(1, 0, n_far, functools.partial(advance, 1, 1))
-        move("z", 1)
+        query(1, 0, n_far // 2)
+        advance(1, 1)
+    move("zr", 1)
     for h in range(hp):
         complete(h)
     attend(0, 0, n_far)
-    advance(1, 2)
-    for ch in range(CHUNKS):
-        move("x", ch)
-        move("z", ch)
+    if pairs > 1:
+        query(1, n_far // 2, n_far)
+        advance(1, 2)
+    move("zr", 2)
     query(0, n_far, groups)
     move("y")
-    move("zr", 0)
+    move("zr", 3)
     if pairs > 1:
         query(1, n_far, groups)
         for h in range(hp, heads):
             complete(h)
         attend(1, 0, n_far)
-    move("zr", 1)
+    move("d")
     attend(0, n_far, groups)
-    move("zr", 2)
     if pairs > 1:
         attend(1, n_far, groups)
-    move("zr", 3)
 
     own = pl.ds(pl.multiple_of(mp * rows, rows), rows)
     partner = source(0, 1)
@@ -524,10 +532,6 @@
         cols = pl.ds(pl.multiple_of(i * nb, nb), nb)
         acc[:, cols] = far_sum(slice(0, rows), slice(0, cut), cols)
 
-    def out_copy(part):
-        at = pl.ds(part * QB, QB)
-        return pltpu.make_async_copy(outv.at[at], out_hbm.at[at], out_sem.at[part])
-
     for part in range(n_parts):
         for r in far:
             for h in range(early, heads):
@@ -539,7 +543,6 @@
             cols = pl.ds(pl.multiple_of(i * nb, nb), nb)
             outv[at, cols] = far_sum(at, slice(cut, width), cols).astype(BF16)
 
-        out_copy(part).start()
 
     own_part(mp).wait_send()
     for ix in remote:
@@ -557,8 +560,6 @@
         for part in range(n_parts):
             for h in range(heads):
                 a_send(r, peer(r // CORES, r % CORES), part, h).wait_send()
-    for part in range(n_parts):
-        out_copy(part).wait()
 
 
 def body(tokens, w_proj, gain, level_codes, w_codes, block_exponent):
@@ -585,9 +586,9 @@
     n_a = groups * (rows // QB) * heads
     return pl.pallas_call(
         functools.partial(kernel, (groups, seq_bits, block_bits, in_bits, factors)),
-        out_shape=jax.ShapeDtypeStruct((rows, depth), BF16),
+        out_shape=pltpu.VMEM((rows, depth), BF16),
         in_specs=[hbm, hbm, hbm, hbm, hbm, pl.BlockSpec(memory_space=pltpu.SMEM)],
-        out_specs=hbm,
+        out_specs=pl.BlockSpec(memory_space=pltpu.VMEM),
         scratch_shapes=[
             pltpu.VMEM((rows_all, depth), BF16),
             pltpu.VMEM((2, depth, 4, pw), BF16),
@@ -604,17 +605,16 @@
             pltpu.VMEM((seq_bits, heads, HEAD_DIM, HEAD_DIM), BF16),
             pltpu.VMEM((in_bits, QB // 2, QB // 2), F32),
             pltpu.VMEM((rows, depth), F32),
-            pltpu.VMEM((rows, depth), BF16),
             pltpu.VMEM(level_codes.shape, jnp.int32),
             pltpu.VMEM((1, width), F32),
-            dma((4,)), dma((2, 4)), dma((QUARTERS,)), dma((2,)), dma((rows // QB,)),
+            dma((4,)), dma((2, 4)), dma((QUARTERS,)), dma((2,)),
             dma((n_w,)), dma((n_w,)),
             dma((n_a,)), dma((n_a,)),
             dma((seq_bits, heads)), dma((seq_bits, heads)),
         ]
         + [pltpu.VMEM((2, depth, 2 * pw), BF16)] * pairs,
         compiler_params=pltpu.CompilerParams(
-            collective_id=0, has_side_effects=True, vmem_limit_bytes=67043328
+            collective_id=0, has_side_effects=True, vmem_limit_bytes=60 * 2**20
         ),
         name="layer",
     )(tokens, w_proj, w_codes, gain.reshape(1, width), level_codes, block_exponent)

time: 59.3 us -> 58.9 us (level); the launches traced: 59.1 us -> 58 us
  local copies, waits for them, and re-layouts: 3.16 us -> 1.32 us
  Pallas kernels: 55.9 us -> 56.7 us
    unnamed x1, local copies, waits for them, and re-layouts: 3.16 us -> 1.32 us
    pallas_call x1, Pallas kernels: 55.9 us -> 56.7 us  [body(): pl.pallas_call(functools.partial(kernel, (groups, seq_bits, block_bits, i...]
where the time goes in v2:
time: 58.9 us; the launch traced here: 58 us
  Pallas kernels  56.7 us (96%)
  local copies, waits for them, and re-layouts  1.32 us (2%)
    pallas_call x1, Pallas kernels, body(): pl.pallas_call(functools.partial(kernel, (groups, seq_bits, block_bits, i...  56.7 us
    unnamed x1, local copies, waits for them, and re-layouts  1.32 us

profile of v2, /device:TPU:0, one launch (start us, length us, event | category | flops | bytes accessed | tf_op | source)
XLA Modules:
  0.0 58.0 jit_solution(18215060213933587014)
XLA Ops:
  0.0 56.7 %layer.1 = bf16[512,2048]{1,0:T(8,128)(2,1)S(1)} custom-call(bf16[2048,2048]{1,0:T(8,128)(2,1)} %tok_hbm.1, bf16[2048,4,512]{2,1,0:T(4,128)(2,1)} %w_hbm.1, s32[512,2048]{1,0:T(8,128)} %codes_hbm.1, f32[1,512]{1,0:T(1,128)} %bitcast.1, s32[9,4,2048]{2,1,0:T(4,128)} %lw_hbm.1, s32[4,16]{1,0:T(4,128)} %scale_ref.1), custom_call_target="tpu_custom_call" | custom-call | tf_op jit(solution)/shard_map/layer/pallas_call | solution.py:587
  56.7 1.3 %copy.8 = bf16[512,2048]{1,0:T(8,128)(2,1)} copy(bf16[512,2048]{1,0:T(8,128)(2,1)S(1)} %layer.1) | data formatting | bytes 4194304
